TPU v7x, 256 devices: a whole 4x4x8 slice. The times are simulated.
256 devices in a mesh: pipe: 16 (over z, core), seq: 4 (over y), batch: 4 (over x).
Axes of the slice: x: 4, y: 4, z: 8, core: 2. Of those that a mesh axis runs over, the one named last changes fastest.
Arguments:
- latent: bfloat16 [32, 32, 2560], P('batch', 'seq'), parts along dimension 0, may hold values from -6 to 6
- w_qkv: bfloat16 [16, 2560, 3, 2560], P('pipe', None, None, 'seq')
- modulation: float32 [16, 8, 3, 2560], P('pipe'), may hold values from -3 to 3
- timestep: int32 [1], replicated, may hold values from 0 to 7
- order: int32 [32], P('batch'), parts along dimension 0, may hold values from 0 to 7, each once
- tiles: int32 [64, 6], P('batch'), parts along dimension 0, may hold values from 0 to 15, as said below
- stale_kv: bfloat16 [16, 32, 32, 2, 2560], P('pipe', 'batch', None, None, 'seq'), parts along dimension 1, may hold values from -6 to 6
Outputs:
- section_out: bfloat16 [16, 32, 32, 2560], P('pipe', 'batch', 'seq'), parts along dimension 1
There are 4 independent parts, one for each index of `batch`. A program takes and returns all parts, laid end to end along the dimension named above; an argument that names none is the same for every part. Nothing has to cross between parts.
Inputs may be any that keep to these rules, and one draw needn't show every extreme that they name: Row g lists tile g first, then 6 - 1 distinct other tiles whose index differs from g modulo 16 by 1 to 5.
All inputs are finite; a program needn't handle non-finite values.
Results may differ from a plain program's by a relative error of at most 0.019.
Values may be sent and summed in bfloat16 or wider, within the bound.
No kernel may reach another device: no remote copies, remote signals or barrier semaphores. Data moves between devices by JAX's collectives and lax.ppermute only.
A program may use at most 128 MiB of HBM per device.

v0:
```python
import functools

import jax
import jax.numpy as jnp
from jax import lax
from jax.experimental import pallas as pl
from jax.experimental.pallas import tpu as pltpu
from jax.sharding import PartitionSpec as P


HEAD_DIM = 128
TILES_P = 2
epsilon = 1e-06
MASKED = -3.0e38
CHUNKS = 4
SEND_ORDER = (2, 1, 3, 0)


def attend_kernel(
    parity,
    chunks,
    scalars,
    order,
    fresh,
    own_rows,
    chosen,
    gate_row,
    kv_before,
    results_before,
    out,
    kv,
    results,
    projected,
    own_buf,
    kv_buf,
    code_buf,
    gate_buf,
    out_buf,
    misc_sem,
):
    rows, local_w = own_buf.shape
    per_chunk = order.shape[0] // chunks
    patch_tok = rows // per_chunk
    age = 2 * scalars[0] + parity - scalars[1]
    chunk = lax.div(age, 2)
    active = (age >= 0) & (lax.rem(age, 2) == 0) & (chunk < chunks)

    @pl.when(active)
    def _():
        patch_rows = []
        for i in range(per_chunk):
            patch = order[chunk * per_chunk + i]
            patch_rows.append(pl.ds(pl.multiple_of(patch * patch_tok, patch_tok), patch_tok))
        loads = [
            pltpu.make_async_copy(fresh, projected, misc_sem.at[0]),
            pltpu.make_async_copy(own_rows, own_buf, misc_sem.at[1]),
            pltpu.make_async_copy(gate_row, gate_buf, misc_sem.at[2]),
        ]
        for i in range(per_chunk):
            loads.append(pltpu.make_async_copy(kv_before, kv_buf.at[i], misc_sem.at[3 + i]))
            loads.append(
                pltpu.make_async_copy(
                    chosen.at[patch_rows[i]], code_buf.at[i], misc_sem.at[3 + per_chunk + i]
                )
            )
        for copy in loads:
            copy.start()
        for copy in loads:
            copy.wait()

        gate = gate_buf[...]
        nt = (((1,), (1,)), ((), ()))
        heads = local_w // HEAD_DIM
        chunk_at = [pl.ds(i * patch_tok, patch_tok) for i in range(per_chunk)]
        head_at = [pl.ds(head * HEAD_DIM, HEAD_DIM) for head in range(heads)]
        backs = []
        chances = []
        for i in range(per_chunk):
            for j in range(i + 1):
                for part in range(2):
                    kv_buf[i, part, patch_rows[j], :] = projected[1 + part, chunk_at[j], :]
        for i in range(per_chunk):
            for part in range(2):
                backs.append(
                    pltpu.make_async_copy(
                        projected.at[1 + part, chunk_at[i]],
                        kv.at[part, patch_rows[i]],
                        misc_sem.at[3 + 2 * per_chunk + 2 * i + part],
                    )
                )
                backs[-1].start()
            scores = jnp.concatenate(
                [
                    lax.dot_general(
                        projected[0, chunk_at[i], cols],
                        kv_buf[i, 0, :, cols],
                        nt,
                        preferred_element_type=jnp.float32,
                    )
                    for cols in head_at
                ],
                axis=0,
            )
            attended = jnp.concatenate([code_buf[i] > 0.5] * heads, axis=0)
            scores = jnp.where(attended, scores * HEAD_DIM ** (-0.5), MASKED)
            largest = jnp.max(scores, axis=-1, keepdims=True)
            raised = jnp.exp(scores - largest)
            total = jnp.sum(raised, axis=-1, keepdims=True)
            chances.append((raised * (1.0 / total)).astype(jnp.bfloat16))
        for i in range(per_chunk):
            for head, cols in enumerate(head_at):
                mixed = jnp.dot(
                    chances[i][head * patch_tok : (head + 1) * patch_tok],
                    kv_buf[i, 1, :, cols],
                    preferred_element_type=jnp.float32,
                )
                mixed = mixed.astype(jnp.bfloat16).astype(jnp.float32)
                own = own_buf[chunk_at[i], cols].astype(jnp.float32)
                gate_part = gate[:, head * HEAD_DIM : (head + 1) * HEAD_DIM]
                out_buf[chunk_at[i], cols] = (own + gate_part * mixed).astype(jnp.bfloat16)
        backs.append(pltpu.make_async_copy(out_buf, out, misc_sem.at[0]))
        backs[-1].start()
        for i in range(per_chunk):
            backs.append(
                pltpu.make_async_copy(
                    out_buf.at[pl.ds(i * patch_tok, patch_tok)],
                    results.at[patch_rows[i]],
                    misc_sem.at[3 + i],
                )
            )
            backs[-1].start()
        for copy in backs:
            copy.wait()


def keep_in_vmem(parity, scalars, value, after):
    def body(scalars, src, after, dst, sem):
        @pl.when(lax.rem(scalars[1], 2) == parity)
        def _():
            copy = pltpu.make_async_copy(src, dst, sem)
            copy.start()
            copy.wait()

    any_spec = pl.BlockSpec(memory_space=pl.ANY)
    return pl.pallas_call(
        body,
        out_shape=pltpu.VMEM(value.shape, value.dtype),
        in_specs=[pl.BlockSpec(memory_space=pltpu.SMEM), any_spec, any_spec],
        out_specs=any_spec,
        scratch_shapes=[pltpu.SemaphoreType.DMA(())],
        compiler_params=pltpu.CompilerParams(vmem_limit_bytes=1024 * 1024),
        name="keep",
    )(scalars, value, after)


def run_attend(parity, chunks, scalars, order, fresh, own, chosen, gate, kv, results):
    per_chunk = order.shape[0] // chunks
    any_spec = pl.BlockSpec(memory_space=pl.ANY)
    smem_spec = pl.BlockSpec(memory_space=pltpu.SMEM)
    return pl.pallas_call(
        functools.partial(attend_kernel, parity, chunks),
        out_shape=(
            jax.ShapeDtypeStruct(own.shape, jnp.bfloat16),
            jax.ShapeDtypeStruct(kv.shape, kv.dtype),
            jax.ShapeDtypeStruct(results.shape, results.dtype),
        ),
        in_specs=[smem_spec] * 2 + [any_spec] * 6,
        out_specs=(any_spec,) * 3,
        scratch_shapes=[
            pltpu.VMEM(fresh.shape, jnp.bfloat16),
            pltpu.VMEM(own.shape, jnp.bfloat16),
            pltpu.VMEM((per_chunk, *kv.shape), jnp.bfloat16),
            pltpu.VMEM((per_chunk, own.shape[0] // per_chunk, chosen.shape[1]), jnp.float32),
            pltpu.VMEM(gate.shape, jnp.float32),
            pltpu.VMEM(own.shape, jnp.bfloat16),
            pltpu.SemaphoreType.DMA((3 + 4 * per_chunk,)),
        ],
        input_output_aliases={6: 1, 7: 2},
        compiler_params=pltpu.CompilerParams(vmem_limit_bytes=12 * 1024 * 1024),
        name="attend",
    )(scalars, order, fresh, own, chosen, gate, kv, results)


def normalize(rows, shift_row, scale_row):
    floated = rows.astype(jnp.float32)
    average = jnp.mean(floated, axis=-1, keepdims=True)
    centred = floated - average
    spread = jnp.mean(centred * centred, axis=-1, keepdims=True)
    return (centred * lax.rsqrt(spread + epsilon) * (1.0 + scale_row) + shift_row).astype(
        jnp.bfloat16
    )


def pair_list(pipe_count, seq_count, parity, by):
    return [
        (s * seq_count + q, (s + 1) * seq_count + (q + by) % seq_count)
        for s in range(parity, pipe_count - 1, 2)
        for q in range(seq_count)
    ]


def chosen_keys(tiles, tile_len):
    n_tiles = tiles.shape[0]
    tile_ids = jnp.arange(n_tiles, dtype=jnp.int32)
    chosen = jnp.any(tiles[:, :, None] == tile_ids[None, None, :], axis=1).astype(jnp.float32)
    return jnp.repeat(jnp.repeat(chosen, tile_len, 0), tile_len, 1)


def local(latent, w_qkv, modulation, timestep, order, tiles, stale_kv):
    patches, rows_dev, width = latent.shape
    local_w = w_qkv.shape[3]
    seq_count = lax.axis_size("seq")
    pipe_count = lax.axis_size("pipe")
    section_rank = lax.axis_index("pipe").astype(jnp.int32)
    seq_rank = lax.axis_index("seq").astype(jnp.int32)
    patch_tok = rows_dev * seq_count
    rows = patches * patch_tok
    chunk_rows = rows // CHUNKS
    weights = jnp.transpose(w_qkv[0], (1, 0, 2))
    mod_rows = lax.dynamic_index_in_dim(modulation[0], timestep[0], 0, keepdims=False)
    gate = lax.dynamic_slice_in_dim(mod_rows[2:], seq_rank * local_w, local_w, 1)
    kv = jnp.moveaxis(stale_kv[0], 2, 0).reshape(2, rows, local_w)
    chosen = chosen_keys(tiles, patch_tok // TILES_P)

    quarters = [latent] + [
        lax.ppermute(
            latent, ("pipe", "seq"), [(q, (q + by) % seq_count) for q in range(seq_count)]
        )
        for by in range(1, seq_count)
    ]
    tokens = jnp.stack(
        [lax.select_n((seq_rank + seq_count - j) % seq_count, *quarters) for j in range(seq_count)],
        axis=1,
    ).reshape(patches, patch_tok, width)[order]
    tokens = tokens.reshape(CHUNKS, chunk_rows, width)

    def send(out, parity):
        arrived = [None] * seq_count
        for by in SEND_ORDER:
            arrived[by] = lax.ppermute(
                out, ("pipe", "seq"), pair_list(pipe_count, seq_count, parity, by)
            )
        return tuple(arrived)

    def two_turns(i, carry):
        out, kv, results = carry
        scalars = jnp.stack([i, section_rank, seq_rank])
        for parity in range(2):
            pieces = send(out, 1 - parity)
            held = keep_in_vmem(parity, scalars, weights, out)
            whole = jnp.concatenate(
                [lax.select_n((seq_rank + seq_count - j) % seq_count, *pieces) for j in range(seq_count)],
                axis=1,
            )
            own = pieces[0]
            if parity == 0:
                chunk = jnp.clip(i, 0, CHUNKS - 1)
                entry = lax.dynamic_index_in_dim(tokens, chunk, 0, keepdims=False)
                whole = jnp.where(section_rank == 0, entry, whole)
                entry = lax.dynamic_slice(
                    tokens, (chunk, 0, seq_rank * local_w), (1, chunk_rows, local_w)
                )[0]
                own = jnp.where(section_rank == 0, entry, own)
            normed = normalize(whole, mod_rows[0], mod_rows[1])
            fresh = lax.dot_general(
                normed, held, (((1,), (1,)), ((), ())), preferred_element_type=jnp.float32
            ).astype(jnp.bfloat16)
            fresh = jnp.moveaxis(fresh, 1, 0)
            out, kv, results = run_attend(
                parity, CHUNKS, scalars, order, fresh, own, chosen, gate, kv, results
            )
        return out, kv, results

    turns = pipe_count + 2 * (CHUNKS - 1)
    _, kv, results = lax.fori_loop(
        0,
        (turns + 1) // 2,
        two_turns,
        (
            jnp.zeros((chunk_rows, local_w), jnp.bfloat16),
            kv,
            jnp.zeros((rows, local_w), jnp.bfloat16),
        ),
    )
    columns = results.reshape(patches, patch_tok, local_w)
    finished = lax.all_to_all(columns, "seq", split_axis=1, concat_axis=2, tiled=True)
    return finished[None]


def solution(mesh):
    return jax.shard_map(
        local,
        mesh=mesh,
        in_specs=(
            P("batch", "seq", None),
            P("pipe", None, None, "seq"),
            P("pipe", None, None, None),
            P(),
            P("batch"),
            P("batch", None),
            P("pipe", "batch", None, None, "seq"),
        ),
        out_specs=P("pipe", "batch", "seq", None),
        check_vma=False,
    )
```

profile of v0, /device:TPU:225, one launch (start us, length us, event | category | flops | bytes accessed | tf_op | source)
XLA Modules:
  0.0 339.2 jit_solution(17357633378847861952)
XLA Ops:
  7.0 323.1 %while.20 = (s32[]{:T(128)}, bf16[64,640]{1,0:T(8,128)(2,1)S(1)}, bf16[2,256,640]{2,1,0:T(8,128)(2,1)S(1)}, bf16[256,640]{1,0:T(8,128)(2,1)S(1)}, s32[]{:T(128)}...) while((s32[]{:T(128)}, bf16[64,640]{1,0:T(8,128)(2,1)S(1)}, ...), condition=%wide.region_6.7_spmd.clone, body=%wide.region_1.6_spmd.clone.sunk | while | flops 1268411008 | bytes 27964592 | solution.py:275
  19.2 4.4 %keep.15 = bf16[3,2560,640]{2,1,0:T(8,128)(2,1)S(1)} custom-call(s32[3]{0:T(128)S(1)} %pad_add_fusion.2.scalars, bf16[3,2560,640]{2,1,0:T(8,128)(2,1)} %get-tuple-element.789.src, bf16[64,640]{1,0:T(8,128)(2,1)S(1)} %get-tuple-element.700.after), custom_call_target="tpu_custom_call" | custom-call | tf_op jit(solution)/shard_map/while/body/eval_jaxpr/keep/pallas_call | solution.py:145
  23.6 5.3 %collective-permute-done.7 = bf16[64,640]{1,0:T(8,128)(2,1)S(1)} collective-permute-done((bf16[64,640]{1,0:T(8,128)(2,1)S(1)}, bf16[64,640]{1,0:T(8,128)(2,1)S(1)}, u32[]{:S(2)}, u32[]{:S(2)}) %collective-permute-start.7) | collective-permute-done | bytes 81952 | tf_op jit(solution)/shard_map/while/body/eval_jaxpr/ppermute | solution.py:240
  47.3 4.4 %keep.15 = bf16[3,2560,640]{2,1,0:T(8,128)(2,1)S(1)} custom-call(s32[3]{0:T(128)S(1)} %pad_add_fusion.2.scalars, bf16[3,2560,640]{2,1,0:T(8,128)(2,1)} %get-tuple-element.789.src, bf16[64,640]{1,0:T(8,128)(2,1)S(1)} %get-tuple-element.700.after), custom_call_target="tpu_custom_call" | custom-call | tf_op jit(solution)/shard_map/while/body/eval_jaxpr/keep/pallas_call | solution.py:145
  72.2 4.4 %keep.15 = bf16[3,2560,640]{2,1,0:T(8,128)(2,1)S(1)} custom-call(s32[3]{0:T(128)S(1)} %pad_add_fusion.2.scalars, bf16[3,2560,640]{2,1,0:T(8,128)(2,1)} %get-tuple-element.789.src, bf16[64,640]{1,0:T(8,128)(2,1)S(1)} %get-tuple-element.700.after), custom_call_target="tpu_custom_call" | custom-call | tf_op jit(solution)/shard_map/while/body/eval_jaxpr/keep/pallas_call | solution.py:145
  76.5 2.8 collective-permute-done.7
  97.6 4.4 %keep.15 = bf16[3,2560,640]{2,1,0:T(8,128)(2,1)S(1)} custom-call(s32[3]{0:T(128)S(1)} %pad_add_fusion.2.scalars, bf16[3,2560,640]{2,1,0:T(8,128)(2,1)} %get-tuple-element.789.src, bf16[64,640]{1,0:T(8,128)(2,1)S(1)} %get-tuple-element.700.after), custom_call_target="tpu_custom_call" | custom-call | tf_op jit(solution)/shard_map/while/body/eval_jaxpr/keep/pallas_call | solution.py:145
  102.0 2.6 collective-permute-done.7
  122.8 4.4 %keep.15 = bf16[3,2560,640]{2,1,0:T(8,128)(2,1)S(1)} custom-call(s32[3]{0:T(128)S(1)} %pad_add_fusion.2.scalars, bf16[3,2560,640]{2,1,0:T(8,128)(2,1)} %get-tuple-element.789.src, bf16[64,640]{1,0:T(8,128)(2,1)S(1)} %get-tuple-element.700.after), custom_call_target="tpu_custom_call" | custom-call | tf_op jit(solution)/shard_map/while/body/eval_jaxpr/keep/pallas_call | solution.py:145
  127.2 2.6 collective-permute-done.7
  148.1 4.4 %keep.15 = bf16[3,2560,640]{2,1,0:T(8,128)(2,1)S(1)} custom-call(s32[3]{0:T(128)S(1)} %pad_add_fusion.2.scalars, bf16[3,2560,640]{2,1,0:T(8,128)(2,1)} %get-tuple-element.789.src, bf16[64,640]{1,0:T(8,128)(2,1)S(1)} %get-tuple-element.700.after), custom_call_target="tpu_custom_call" | custom-call | tf_op jit(solution)/shard_map/while/body/eval_jaxpr/keep/pallas_call | solution.py:145
  152.5 2.6 collective-permute-done.7
  173.7 4.4 %keep.15 = bf16[3,2560,640]{2,1,0:T(8,128)(2,1)S(1)} custom-call(s32[3]{0:T(128)S(1)} %pad_add_fusion.2.scalars, bf16[3,2560,640]{2,1,0:T(8,128)(2,1)} %get-tuple-element.789.src, bf16[64,640]{1,0:T(8,128)(2,1)S(1)} %get-tuple-element.700.after), custom_call_target="tpu_custom_call" | custom-call | tf_op jit(solution)/shard_map/while/body/eval_jaxpr/keep/pallas_call | solution.py:145
  178.0 2.9 collective-permute-done.7
  181.7 3.1 collective-permute-done.4
  200.1 4.4 %keep.15 = bf16[3,2560,640]{2,1,0:T(8,128)(2,1)S(1)} custom-call(s32[3]{0:T(128)S(1)} %pad_add_fusion.2.scalars, bf16[3,2560,640]{2,1,0:T(8,128)(2,1)} %get-tuple-element.789.src, bf16[64,640]{1,0:T(8,128)(2,1)S(1)} %get-tuple-element.700.after), custom_call_target="tpu_custom_call" | custom-call | tf_op jit(solution)/shard_map/while/body/eval_jaxpr/keep/pallas_call | solution.py:145
  204.5 30.0 %collective-permute-done.7 = bf16[64,640]{1,0:T(8,128)(2,1)S(1)} collective-permute-done((bf16[64,640]{1,0:T(8,128)(2,1)S(1)}, bf16[64,640]{1,0:T(8,128)(2,1)S(1)}, u32[]{:S(2)}, u32[]{:S(2)}) %collective-permute-start.7) | collective-permute-done | bytes 81952 | tf_op jit(solution)/shard_map/while/body/eval_jaxpr/ppermute | solution.py:240
  235.3 3.2 collective-permute-done.4
  240.9 3.0 attend.15
  256.0 4.4 %keep.15 = bf16[3,2560,640]{2,1,0:T(8,128)(2,1)S(1)} custom-call(s32[3]{0:T(128)S(1)} %pad_add_fusion.2.scalars, bf16[3,2560,640]{2,1,0:T(8,128)(2,1)} %get-tuple-element.789.src, bf16[64,640]{1,0:T(8,128)(2,1)S(1)} %get-tuple-element.700.after), custom_call_target="tpu_custom_call" | custom-call | tf_op jit(solution)/shard_map/while/body/eval_jaxpr/keep/pallas_call | solution.py:145
  260.4 2.9 collective-permute-done.7
  264.1 3.1 collective-permute-done.4
  269.6 3.0 attend.15
  284.8 4.4 %keep.15 = bf16[3,2560,640]{2,1,0:T(8,128)(2,1)S(1)} custom-call(s32[3]{0:T(128)S(1)} %pad_add_fusion.2.scalars, bf16[3,2560,640]{2,1,0:T(8,128)(2,1)} %get-tuple-element.789.src, bf16[64,640]{1,0:T(8,128)(2,1)S(1)} %get-tuple-element.700.after), custom_call_target="tpu_custom_call" | custom-call | tf_op jit(solution)/shard_map/while/body/eval_jaxpr/keep/pallas_call | solution.py:145
  289.1 2.9 collective-permute-done.7
  292.9 3.1 collective-permute-done.4
  298.4 3.0 attend.15
  313.5 4.4 %keep.15 = bf16[3,2560,640]{2,1,0:T(8,128)(2,1)S(1)} custom-call(s32[3]{0:T(128)S(1)} %pad_add_fusion.2.scalars, bf16[3,2560,640]{2,1,0:T(8,128)(2,1)} %get-tuple-element.789.src, bf16[64,640]{1,0:T(8,128)(2,1)S(1)} %get-tuple-element.700.after), custom_call_target="tpu_custom_call" | custom-call | tf_op jit(solution)/shard_map/while/body/eval_jaxpr/keep/pallas_call | solution.py:145
  317.9 2.9 collective-permute-done.7
  321.6 3.1 collective-permute-done.4
  327.1 3.0 attend.15
  330.2 8.3 %all_to_all.15 = bf16[8,32,640]{2,0,1:T(8,128)(2,1)S(1)} all-to-all(bf16[8,32,640]{2,0,1:T(8,128)(2,1)S(1)} %copy.45), channel_id=1, replica_groups=mesh['pipe'=16,'seq'=4,'batch'=4] {'seq'}, dimensions={1} | all-to-all | bytes 655360 | tf_op jit(solution)/shard_map/all_to_all | solution.py:286
  (429 shorter events, 194.9 us)
Async XLA Ops:
  14.0 14.8 %collective-permute-start.7 = (bf16[64,640]{1,0:T(8,128)(2,1)S(1)}, bf16[64,640]{1,0:T(8,128)(2,1)S(1)}, u32[]{:S(2)}, u32[]{:S(2)}) collective-permute-start(bf16[64,640]{1,0:T(8,128)(2,1)S(1)} %get-tuple-element.700.after), channel_id=1, source_target_pairs={{0,20},{4,24},{8,28},{12,16},{32,52},{36,56},{40,60},{44,48},{64,8... | collective-permute-start | bytes 245768 | tf_op jit(solution)/shard_map/while/body/eval_jaxpr/ppermute | solution.py:240
  15.3 13.5 %collective-permute-start.6 = (bf16[64,640]{1,0:T(8,128)(2,1)S(1)}, bf16[64,640]{1,0:T(8,128)(2,1)S(1)}, u32[]{:S(2)}, u32[]{:S(2)}) collective-permute-start(bf16[64,640]{1,0:T(8,128)(2,1)S(1)} %get-tuple-element.700.after), channel_id=1, source_target_pairs={{0,16},{4,20},{8,24},{12,28},{32,48},{36,52},{40,56},{44,60},{64,8... | collective-permute-start | bytes 245768 | tf_op jit(solution)/shard_map/while/body/eval_jaxpr/ppermute | solution.py:240
  16.6 12.8 %collective-permute-start.5 = (bf16[64,640]{1,0:T(8,128)(2,1)S(1)}, bf16[64,640]{1,0:T(8,128)(2,1)S(1)}, u32[]{:S(2)}, u32[]{:S(2)}) collective-permute-start(bf16[64,640]{1,0:T(8,128)(2,1)S(1)} %get-tuple-element.700.after), channel_id=1, source_target_pairs={{0,28},{4,16},{8,20},{12,24},{32,60},{36,48},{40,52},{44,56},{64,9... | collective-permute-start | bytes 245768 | tf_op jit(solution)/shard_map/while/body/eval_jaxpr/ppermute | solution.py:240
  17.9 14.1 %collective-permute-start.4 = (bf16[64,640]{1,0:T(8,128)(2,1)S(1)}, bf16[64,640]{1,0:T(8,128)(2,1)S(1)}, u32[]{:S(2)}, u32[]{:S(2)}) collective-permute-start(bf16[64,640]{1,0:T(8,128)(2,1)S(1)} %get-tuple-element.700.after), channel_id=1, source_target_pairs={{0,24},{4,28},{8,16},{12,20},{32,56},{36,60},{40,48},{44,52},{64,8... | collective-permute-start | bytes 245768 | tf_op jit(solution)/shard_map/while/body/eval_jaxpr/ppermute | solution.py:240
  42.1 12.0 %collective-permute-start.7 = (bf16[64,640]{1,0:T(8,128)(2,1)S(1)}, bf16[64,640]{1,0:T(8,128)(2,1)S(1)}, u32[]{:S(2)}, u32[]{:S(2)}) collective-permute-start(bf16[64,640]{1,0:T(8,128)(2,1)S(1)} %get-tuple-element.700.after), channel_id=1, source_target_pairs={{0,20},{4,24},{8,28},{12,16},{32,52},{36,56},{40,60},{44,48},{64,8... | collective-permute-start | bytes 245768 | tf_op jit(solution)/shard_map/while/body/eval_jaxpr/ppermute | solution.py:240
  46.0 10.9 %collective-permute-start.4 = (bf16[64,640]{1,0:T(8,128)(2,1)S(1)}, bf16[64,640]{1,0:T(8,128)(2,1)S(1)}, u32[]{:S(2)}, u32[]{:S(2)}) collective-permute-start(bf16[64,640]{1,0:T(8,128)(2,1)S(1)} %get-tuple-element.700.after), channel_id=1, source_target_pairs={{0,24},{4,28},{8,16},{12,20},{32,56},{36,60},{40,48},{44,52},{64,8... | collective-permute-start | bytes 245768 | tf_op jit(solution)/shard_map/while/body/eval_jaxpr/ppermute | solution.py:240
  67.0 12.4 %collective-permute-start.7 = (bf16[64,640]{1,0:T(8,128)(2,1)S(1)}, bf16[64,640]{1,0:T(8,128)(2,1)S(1)}, u32[]{:S(2)}, u32[]{:S(2)}) collective-permute-start(bf16[64,640]{1,0:T(8,128)(2,1)S(1)} %get-tuple-element.700.after), channel_id=1, source_target_pairs={{0,20},{4,24},{8,28},{12,16},{32,52},{36,56},{40,60},{44,48},{64,8... | collective-permute-start | bytes 245768 | tf_op jit(solution)/shard_map/while/body/eval_jaxpr/ppermute | solution.py:240
  68.3 11.1 %collective-permute-start.6 = (bf16[64,640]{1,0:T(8,128)(2,1)S(1)}, bf16[64,640]{1,0:T(8,128)(2,1)S(1)}, u32[]{:S(2)}, u32[]{:S(2)}) collective-permute-start(bf16[64,640]{1,0:T(8,128)(2,1)S(1)} %get-tuple-element.700.after), channel_id=1, source_target_pairs={{0,16},{4,20},{8,24},{12,28},{32,48},{36,52},{40,56},{44,60},{64,8... | collective-permute-start | bytes 245768 | tf_op jit(solution)/shard_map/while/body/eval_jaxpr/ppermute | solution.py:240
  70.9 11.5 %collective-permute-start.4 = (bf16[64,640]{1,0:T(8,128)(2,1)S(1)}, bf16[64,640]{1,0:T(8,128)(2,1)S(1)}, u32[]{:S(2)}, u32[]{:S(2)}) collective-permute-start(bf16[64,640]{1,0:T(8,128)(2,1)S(1)} %get-tuple-element.700.after), channel_id=1, source_target_pairs={{0,24},{4,28},{8,16},{12,20},{32,56},{36,60},{40,48},{44,52},{64,8... | collective-permute-start | bytes 245768 | tf_op jit(solution)/shard_map/while/body/eval_jaxpr/ppermute | solution.py:240
  92.4 12.2 %collective-permute-start.7 = (bf16[64,640]{1,0:T(8,128)(2,1)S(1)}, bf16[64,640]{1,0:T(8,128)(2,1)S(1)}, u32[]{:S(2)}, u32[]{:S(2)}) collective-permute-start(bf16[64,640]{1,0:T(8,128)(2,1)S(1)} %get-tuple-element.700.after), channel_id=1, source_target_pairs={{0,20},{4,24},{8,28},{12,16},{32,52},{36,56},{40,60},{44,48},{64,8... | collective-permute-start | bytes 245768 | tf_op jit(solution)/shard_map/while/body/eval_jaxpr/ppermute | solution.py:240
  96.3 11.3 %collective-permute-start.4 = (bf16[64,640]{1,0:T(8,128)(2,1)S(1)}, bf16[64,640]{1,0:T(8,128)(2,1)S(1)}, u32[]{:S(2)}, u32[]{:S(2)}) collective-permute-start(bf16[64,640]{1,0:T(8,128)(2,1)S(1)} %get-tuple-element.700.after), channel_id=1, source_target_pairs={{0,24},{4,28},{8,16},{12,20},{32,56},{36,60},{40,48},{44,52},{64,8... | collective-permute-start | bytes 245768 | tf_op jit(solution)/shard_map/while/body/eval_jaxpr/ppermute | solution.py:240
  117.6 12.2 %collective-permute-start.7 = (bf16[64,640]{1,0:T(8,128)(2,1)S(1)}, bf16[64,640]{1,0:T(8,128)(2,1)S(1)}, u32[]{:S(2)}, u32[]{:S(2)}) collective-permute-start(bf16[64,640]{1,0:T(8,128)(2,1)S(1)} %get-tuple-element.700.after), channel_id=1, source_target_pairs={{0,20},{4,24},{8,28},{12,16},{32,52},{36,56},{40,60},{44,48},{64,8... | collective-permute-start | bytes 245768 | tf_op jit(solution)/shard_map/while/body/eval_jaxpr/ppermute | solution.py:240
  118.9 10.9 %collective-permute-start.6 = (bf16[64,640]{1,0:T(8,128)(2,1)S(1)}, bf16[64,640]{1,0:T(8,128)(2,1)S(1)}, u32[]{:S(2)}, u32[]{:S(2)}) collective-permute-start(bf16[64,640]{1,0:T(8,128)(2,1)S(1)} %get-tuple-element.700.after), channel_id=1, source_target_pairs={{0,16},{4,20},{8,24},{12,28},{32,48},{36,52},{40,56},{44,60},{64,8... | collective-permute-start | bytes 245768 | tf_op jit(solution)/shard_map/while/body/eval_jaxpr/ppermute | solution.py:240
  121.5 11.3 %collective-permute-start.4 = (bf16[64,640]{1,0:T(8,128)(2,1)S(1)}, bf16[64,640]{1,0:T(8,128)(2,1)S(1)}, u32[]{:S(2)}, u32[]{:S(2)}) collective-permute-start(bf16[64,640]{1,0:T(8,128)(2,1)S(1)} %get-tuple-element.700.after), channel_id=1, source_target_pairs={{0,24},{4,28},{8,16},{12,20},{32,56},{36,60},{40,48},{44,52},{64,8... | collective-permute-start | bytes 245768 | tf_op jit(solution)/shard_map/while/body/eval_jaxpr/ppermute | solution.py:240
  142.9 12.2 %collective-permute-start.7 = (bf16[64,640]{1,0:T(8,128)(2,1)S(1)}, bf16[64,640]{1,0:T(8,128)(2,1)S(1)}, u32[]{:S(2)}, u32[]{:S(2)}) collective-permute-start(bf16[64,640]{1,0:T(8,128)(2,1)S(1)} %get-tuple-element.700.after), channel_id=1, source_target_pairs={{0,20},{4,24},{8,28},{12,16},{32,52},{36,56},{40,60},{44,48},{64,8... | collective-permute-start | bytes 245768 | tf_op jit(solution)/shard_map/while/body/eval_jaxpr/ppermute | solution.py:240
  146.8 11.6 %collective-permute-start.4 = (bf16[64,640]{1,0:T(8,128)(2,1)S(1)}, bf16[64,640]{1,0:T(8,128)(2,1)S(1)}, u32[]{:S(2)}, u32[]{:S(2)}) collective-permute-start(bf16[64,640]{1,0:T(8,128)(2,1)S(1)} %get-tuple-element.700.after), channel_id=1, source_target_pairs={{0,24},{4,28},{8,16},{12,20},{32,56},{36,60},{40,48},{44,52},{64,8... | collective-permute-start | bytes 245768 | tf_op jit(solution)/shard_map/while/body/eval_jaxpr/ppermute | solution.py:240
  168.5 12.5 %collective-permute-start.7 = (bf16[64,640]{1,0:T(8,128)(2,1)S(1)}, bf16[64,640]{1,0:T(8,128)(2,1)S(1)}, u32[]{:S(2)}, u32[]{:S(2)}) collective-permute-start(bf16[64,640]{1,0:T(8,128)(2,1)S(1)} %get-tuple-element.700.after), channel_id=1, source_target_pairs={{0,20},{4,24},{8,28},{12,16},{32,52},{36,56},{40,60},{44,48},{64,8... | collective-permute-start | bytes 245768 | tf_op jit(solution)/shard_map/while/body/eval_jaxpr/ppermute | solution.py:240
  169.8 11.2 %collective-permute-start.6 = (bf16[64,640]{1,0:T(8,128)(2,1)S(1)}, bf16[64,640]{1,0:T(8,128)(2,1)S(1)}, u32[]{:S(2)}, u32[]{:S(2)}) collective-permute-start(bf16[64,640]{1,0:T(8,128)(2,1)S(1)} %get-tuple-element.700.after), channel_id=1, source_target_pairs={{0,16},{4,20},{8,24},{12,28},{32,48},{36,52},{40,56},{44,60},{64,8... | collective-permute-start | bytes 245768 | tf_op jit(solution)/shard_map/while/body/eval_jaxpr/ppermute | solution.py:240
  172.4 12.5 %collective-permute-start.4 = (bf16[64,640]{1,0:T(8,128)(2,1)S(1)}, bf16[64,640]{1,0:T(8,128)(2,1)S(1)}, u32[]{:S(2)}, u32[]{:S(2)}) collective-permute-start(bf16[64,640]{1,0:T(8,128)(2,1)S(1)} %get-tuple-element.700.after), channel_id=1, source_target_pairs={{0,24},{4,28},{8,16},{12,20},{32,56},{36,60},{40,48},{44,52},{64,8... | collective-permute-start | bytes 245768 | tf_op jit(solution)/shard_map/while/body/eval_jaxpr/ppermute | solution.py:240
  194.9 39.5 %collective-permute-start.7 = (bf16[64,640]{1,0:T(8,128)(2,1)S(1)}, bf16[64,640]{1,0:T(8,128)(2,1)S(1)}, u32[]{:S(2)}, u32[]{:S(2)}) collective-permute-start(bf16[64,640]{1,0:T(8,128)(2,1)S(1)} %get-tuple-element.700.after), channel_id=1, source_target_pairs={{0,20},{4,24},{8,28},{12,16},{32,52},{36,56},{40,60},{44,48},{64,8... | collective-permute-start | bytes 245768 | tf_op jit(solution)/shard_map/while/body/eval_jaxpr/ppermute | solution.py:240
  196.2 38.2 %collective-permute-start.6 = (bf16[64,640]{1,0:T(8,128)(2,1)S(1)}, bf16[64,640]{1,0:T(8,128)(2,1)S(1)}, u32[]{:S(2)}, u32[]{:S(2)}) collective-permute-start(bf16[64,640]{1,0:T(8,128)(2,1)S(1)} %get-tuple-element.700.after), channel_id=1, source_target_pairs={{0,16},{4,20},{8,24},{12,28},{32,48},{36,52},{40,56},{44,60},{64,8... | collective-permute-start | bytes 245768 | tf_op jit(solution)/shard_map/while/body/eval_jaxpr/ppermute | solution.py:240
  197.5 37.8 %collective-permute-start.5 = (bf16[64,640]{1,0:T(8,128)(2,1)S(1)}, bf16[64,640]{1,0:T(8,128)(2,1)S(1)}, u32[]{:S(2)}, u32[]{:S(2)}) collective-permute-start(bf16[64,640]{1,0:T(8,128)(2,1)S(1)} %get-tuple-element.700.after), channel_id=1, source_target_pairs={{0,28},{4,16},{8,20},{12,24},{32,60},{36,48},{40,52},{44,56},{64,9... | collective-permute-start | bytes 245768 | tf_op jit(solution)/shard_map/while/body/eval_jaxpr/ppermute | solution.py:240
  198.8 39.6 %collective-permute-start.4 = (bf16[64,640]{1,0:T(8,128)(2,1)S(1)}, bf16[64,640]{1,0:T(8,128)(2,1)S(1)}, u32[]{:S(2)}, u32[]{:S(2)}) collective-permute-start(bf16[64,640]{1,0:T(8,128)(2,1)S(1)} %get-tuple-element.700.after), channel_id=1, source_target_pairs={{0,24},{4,28},{8,16},{12,20},{32,56},{36,60},{40,48},{44,52},{64,8... | collective-permute-start | bytes 245768 | tf_op jit(solution)/shard_map/while/body/eval_jaxpr/ppermute | solution.py:240
  250.8 12.5 %collective-permute-start.7 = (bf16[64,640]{1,0:T(8,128)(2,1)S(1)}, bf16[64,640]{1,0:T(8,128)(2,1)S(1)}, u32[]{:S(2)}, u32[]{:S(2)}) collective-permute-start(bf16[64,640]{1,0:T(8,128)(2,1)S(1)} %get-tuple-element.700.after), channel_id=1, source_target_pairs={{0,20},{4,24},{8,28},{12,16},{32,52},{36,56},{40,60},{44,48},{64,8... | collective-permute-start | bytes 245768 | tf_op jit(solution)/shard_map/while/body/eval_jaxpr/ppermute | solution.py:240
  252.1 11.2 %collective-permute-start.6 = (bf16[64,640]{1,0:T(8,128)(2,1)S(1)}, bf16[64,640]{1,0:T(8,128)(2,1)S(1)}, u32[]{:S(2)}, u32[]{:S(2)}) collective-permute-start(bf16[64,640]{1,0:T(8,128)(2,1)S(1)} %get-tuple-element.700.after), channel_id=1, source_target_pairs={{0,16},{4,20},{8,24},{12,28},{32,48},{36,52},{40,56},{44,60},{64,8... | collective-permute-start | bytes 245768 | tf_op jit(solution)/shard_map/while/body/eval_jaxpr/ppermute | solution.py:240
  254.7 12.5 %collective-permute-start.4 = (bf16[64,640]{1,0:T(8,128)(2,1)S(1)}, bf16[64,640]{1,0:T(8,128)(2,1)S(1)}, u32[]{:S(2)}, u32[]{:S(2)}) collective-permute-start(bf16[64,640]{1,0:T(8,128)(2,1)S(1)} %get-tuple-element.700.after), channel_id=1, source_target_pairs={{0,24},{4,28},{8,16},{12,20},{32,56},{36,60},{40,48},{44,52},{64,8... | collective-permute-start | bytes 245768 | tf_op jit(solution)/shard_map/while/body/eval_jaxpr/ppermute | solution.py:240
  279.6 12.5 %collective-permute-start.7 = (bf16[64,640]{1,0:T(8,128)(2,1)S(1)}, bf16[64,640]{1,0:T(8,128)(2,1)S(1)}, u32[]{:S(2)}, u32[]{:S(2)}) collective-permute-start(bf16[64,640]{1,0:T(8,128)(2,1)S(1)} %get-tuple-element.700.after), channel_id=1, source_target_pairs={{0,20},{4,24},{8,28},{12,16},{32,52},{36,56},{40,60},{44,48},{64,8... | collective-permute-start | bytes 245768 | tf_op jit(solution)/shard_map/while/body/eval_jaxpr/ppermute | solution.py:240
  280.9 11.2 %collective-permute-start.6 = (bf16[64,640]{1,0:T(8,128)(2,1)S(1)}, bf16[64,640]{1,0:T(8,128)(2,1)S(1)}, u32[]{:S(2)}, u32[]{:S(2)}) collective-permute-start(bf16[64,640]{1,0:T(8,128)(2,1)S(1)} %get-tuple-element.700.after), channel_id=1, source_target_pairs={{0,16},{4,20},{8,24},{12,28},{32,48},{36,52},{40,56},{44,60},{64,8... | collective-permute-start | bytes 245768 | tf_op jit(solution)/shard_map/while/body/eval_jaxpr/ppermute | solution.py:240
  283.5 12.5 %collective-permute-start.4 = (bf16[64,640]{1,0:T(8,128)(2,1)S(1)}, bf16[64,640]{1,0:T(8,128)(2,1)S(1)}, u32[]{:S(2)}, u32[]{:S(2)}) collective-permute-start(bf16[64,640]{1,0:T(8,128)(2,1)S(1)} %get-tuple-element.700.after), channel_id=1, source_target_pairs={{0,24},{4,28},{8,16},{12,20},{32,56},{36,60},{40,48},{44,52},{64,8... | collective-permute-start | bytes 245768 | tf_op jit(solution)/shard_map/while/body/eval_jaxpr/ppermute | solution.py:240
  308.3 12.5 %collective-permute-start.7 = (bf16[64,640]{1,0:T(8,128)(2,1)S(1)}, bf16[64,640]{1,0:T(8,128)(2,1)S(1)}, u32[]{:S(2)}, u32[]{:S(2)}) collective-permute-start(bf16[64,640]{1,0:T(8,128)(2,1)S(1)} %get-tuple-element.700.after), channel_id=1, source_target_pairs={{0,20},{4,24},{8,28},{12,16},{32,52},{36,56},{40,60},{44,48},{64,8... | collective-permute-start | bytes 245768 | tf_op jit(solution)/shard_map/while/body/eval_jaxpr/ppermute | solution.py:240
  309.6 11.2 %collective-permute-start.6 = (bf16[64,640]{1,0:T(8,128)(2,1)S(1)}, bf16[64,640]{1,0:T(8,128)(2,1)S(1)}, u32[]{:S(2)}, u32[]{:S(2)}) collective-permute-start(bf16[64,640]{1,0:T(8,128)(2,1)S(1)} %get-tuple-element.700.after), channel_id=1, source_target_pairs={{0,16},{4,20},{8,24},{12,28},{32,48},{36,52},{40,56},{44,60},{64,8... | collective-permute-start | bytes 245768 | tf_op jit(solution)/shard_map/while/body/eval_jaxpr/ppermute | solution.py:240
  312.2 12.5 %collective-permute-start.4 = (bf16[64,640]{1,0:T(8,128)(2,1)S(1)}, bf16[64,640]{1,0:T(8,128)(2,1)S(1)}, u32[]{:S(2)}, u32[]{:S(2)}) collective-permute-start(bf16[64,640]{1,0:T(8,128)(2,1)S(1)} %get-tuple-element.700.after), channel_id=1, source_target_pairs={{0,24},{4,28},{8,16},{12,20},{32,56},{36,60},{40,48},{44,52},{64,8... | collective-permute-start | bytes 245768 | tf_op jit(solution)/shard_map/while/body/eval_jaxpr/ppermute | solution.py:240
  (73 other events, 289.6 us)
where the time goes:
time: 342 us; the launch traced here: 339 us
  waiting for transfers between devices  98.1 us (29%)
  starting transfers between devices  88.3 us (26%)
  Pallas kernels  77.7 us (23%)
  matrix products  41.7 us (12%)
  other arithmetic  14.3 us (4%)
  blocking collectives  8.25 us (2%)
  local copies, waits for them, and re-layouts  7.68 us (2%)
    ppermute x88, waiting for transfers between devices, send(): lax.ppermute(out, ('pipe', 'seq'), pair_list(pipe_count, seq_count, parit...  98.1 us
    ppermute x88, starting transfers between devices, send(): lax.ppermute(out, ('pipe', 'seq'), pair_list(pipe_count, seq_count, parit...  86.1 us
    pallas_call x22, Pallas kernels, keep_in_vmem(): pl.pallas_call(body, out_shape=pltpu.VMEM(value.shape, value.dtype), in_s...  54 us
    dot_general x22, matrix products, two_turns(): lax.dot_general(normed, held, (((1,), (1,)), ((), ())), preferred_element...  41.7 us
    pallas_call x22, Pallas kernels, run_attend(): pl.pallas_call(functools.partial(attend_kernel, parity, chunks), out_shap...  23.7 us
    all_to_all x1, blocking collectives, local(): lax.all_to_all(columns, 'seq', split_axis=1, concat_axis=2, tiled=True)  8.25 us
  transfers between devices with their start and end apart: 91, of which 33 were waited for; matrix products, arithmetic and copies ran while one was open for 2% of the time, Pallas kernels for 16%

commit v1 on v0

--- a/solution.py
+++ b/solution.py
@@ -282,8 +282,23 @@
             jnp.zeros((rows, local_w), jnp.bfloat16),
         ),
     )
-    columns = results.reshape(patches, patch_tok, local_w)
-    finished = lax.all_to_all(columns, "seq", split_axis=1, concat_axis=2, tiled=True)
+    columns = results.reshape(patches, seq_count, rows_dev, local_w)
+    parts = []
+    for by in range(seq_count):
+        target = (seq_rank + by) % seq_count
+        part = lax.dynamic_index_in_dim(columns, target, 1, keepdims=False)
+        if by:
+            pairs = [
+                (s * seq_count + q, s * seq_count + (q + by) % seq_count)
+                for s in range(pipe_count)
+                for q in range(seq_count)
+            ]
+            part = lax.ppermute(part, ("pipe", "seq"), pairs)
+        parts.append(part)
+    finished = jnp.concatenate(
+        [lax.select_n((seq_rank + seq_count - j) % seq_count, *parts) for j in range(seq_count)],
+        axis=2,
+    )
     return finished[None]
 
 

time: 342 us -> 337 us (0.985)
  the two profiles are of different devices: /device:TPU:225 before, /device:TPU:229 now
where the time goes in v1:
time: 337 us; the launch traced here: 335 us
  waiting for transfers between devices  99 us (29%)
  starting transfers between devices  92.2 us (27%)
  Pallas kernels  77.7 us (23%)
  matrix products  41.7 us (12%)
  other arithmetic  15.4 us (5%)
  local copies, waits for them, and re-layouts  5.22 us (2%)
    ppermute x88, waiting for transfers between devices, send(): lax.ppermute(out, ('pipe', 'seq'), pair_list(pipe_count, seq_count, parit...  96.8 us
    ppermute x88, starting transfers between devices, send(): lax.ppermute(out, ('pipe', 'seq'), pair_list(pipe_count, seq_count, parit...  86.1 us
    pallas_call x22, Pallas kernels, keep_in_vmem(): pl.pallas_call(body, out_shape=pltpu.VMEM(value.shape, value.dtype), in_s...  54 us
    dot_general x22, matrix products, two_turns(): lax.dot_general(normed, held, (((1,), (1,)), ((), ())), preferred_element...  41.7 us
    pallas_call x22, Pallas kernels, run_attend(): pl.pallas_call(functools.partial(attend_kernel, parity, chunks), out_shap...  23.7 us
  transfers between devices with their start and end apart: 94, of which 40 were waited for; matrix products, arithmetic and copies ran while one was open for 1% of the time, Pallas kernels for 16%

profile of v1, /device:TPU:229, one launch (start us, length us, event | category | flops | bytes accessed | tf_op | source)
XLA Modules:
  0.0 334.5 jit_solution(7785010925120400075)
XLA Ops:
  8.2 319.5 %while.20 = (s32[]{:T(128)}, bf16[64,640]{1,0:T(8,128)(2,1)S(1)}, bf16[2,256,640]{2,1,0:T(8,128)(2,1)S(1)}, bf16[256,640]{1,0:T(8,128)(2,1)S(1)}, s32[]{:T(128)}...) while((s32[]{:T(128)}, bf16[64,640]{1,0:T(8,128)(2,1)S(1)}, ...), condition=%wide.region_6.7_spmd.clone, body=%wide.region_1.6_spmd.clone.sunk | while | flops 1268411008 | bytes 27841684 | solution.py:275
  20.1 4.4 %keep.15 = bf16[3,2560,640]{2,1,0:T(8,128)(2,1)S(1)} custom-call(s32[3]{0:T(128)S(1)} %pad_add_fusion.2.scalars, bf16[3,2560,640]{2,1,0:T(8,128)(2,1)} %get-tuple-element.796.src, bf16[64,640]{1,0:T(8,128)(2,1)S(1)} %get-tuple-element.707.after), custom_call_target="tpu_custom_call" | custom-call | tf_op jit(solution)/shard_map/while/body/eval_jaxpr/keep/pallas_call | solution.py:145
  24.5 5.0 %collective-permute-done.4 = bf16[64,640]{1,0:T(8,128)(2,1)S(1)} collective-permute-done((bf16[64,640]{1,0:T(8,128)(2,1)S(1)}, bf16[64,640]{1,0:T(8,128)(2,1)S(1)}, u32[]{:S(2)}, u32[]{:S(2)}) %collective-permute-start.4) | collective-permute-done | bytes 81952 | tf_op jit(solution)/shard_map/while/body/eval_jaxpr/ppermute | solution.py:240
  30.1 2.5 collective-permute-done.7
  47.6 4.4 %keep.15 = bf16[3,2560,640]{2,1,0:T(8,128)(2,1)S(1)} custom-call(s32[3]{0:T(128)S(1)} %pad_add_fusion.2.scalars, bf16[3,2560,640]{2,1,0:T(8,128)(2,1)} %get-tuple-element.796.src, bf16[64,640]{1,0:T(8,128)(2,1)S(1)} %get-tuple-element.707.after), custom_call_target="tpu_custom_call" | custom-call | tf_op jit(solution)/shard_map/while/body/eval_jaxpr/keep/pallas_call | solution.py:145
  55.1 2.7 collective-permute-done.7
  72.8 4.4 %keep.15 = bf16[3,2560,640]{2,1,0:T(8,128)(2,1)S(1)} custom-call(s32[3]{0:T(128)S(1)} %pad_add_fusion.2.scalars, bf16[3,2560,640]{2,1,0:T(8,128)(2,1)} %get-tuple-element.796.src, bf16[64,640]{1,0:T(8,128)(2,1)S(1)} %get-tuple-element.707.after), custom_call_target="tpu_custom_call" | custom-call | tf_op jit(solution)/shard_map/while/body/eval_jaxpr/keep/pallas_call | solution.py:145
  80.3 3.1 collective-permute-done.7
  98.5 4.4 %keep.15 = bf16[3,2560,640]{2,1,0:T(8,128)(2,1)S(1)} custom-call(s32[3]{0:T(128)S(1)} %pad_add_fusion.2.scalars, bf16[3,2560,640]{2,1,0:T(8,128)(2,1)} %get-tuple-element.796.src, bf16[64,640]{1,0:T(8,128)(2,1)S(1)} %get-tuple-element.707.after), custom_call_target="tpu_custom_call" | custom-call | tf_op jit(solution)/shard_map/while/body/eval_jaxpr/keep/pallas_call | solution.py:145
  105.6 3.1 collective-permute-done.7
  123.7 4.4 %keep.15 = bf16[3,2560,640]{2,1,0:T(8,128)(2,1)S(1)} custom-call(s32[3]{0:T(128)S(1)} %pad_add_fusion.2.scalars, bf16[3,2560,640]{2,1,0:T(8,128)(2,1)} %get-tuple-element.796.src, bf16[64,640]{1,0:T(8,128)(2,1)S(1)} %get-tuple-element.707.after), custom_call_target="tpu_custom_call" | custom-call | tf_op jit(solution)/shard_map/while/body/eval_jaxpr/keep/pallas_call | solution.py:145
  130.8 3.1 collective-permute-done.7
  149.0 4.4 %keep.15 = bf16[3,2560,640]{2,1,0:T(8,128)(2,1)S(1)} custom-call(s32[3]{0:T(128)S(1)} %pad_add_fusion.2.scalars, bf16[3,2560,640]{2,1,0:T(8,128)(2,1)} %get-tuple-element.796.src, bf16[64,640]{1,0:T(8,128)(2,1)S(1)} %get-tuple-element.707.after), custom_call_target="tpu_custom_call" | custom-call | tf_op jit(solution)/shard_map/while/body/eval_jaxpr/keep/pallas_call | solution.py:145
  156.0 3.1 collective-permute-done.7
  174.2 4.4 %keep.15 = bf16[3,2560,640]{2,1,0:T(8,128)(2,1)S(1)} custom-call(s32[3]{0:T(128)S(1)} %pad_add_fusion.2.scalars, bf16[3,2560,640]{2,1,0:T(8,128)(2,1)} %get-tuple-element.796.src, bf16[64,640]{1,0:T(8,128)(2,1)S(1)} %get-tuple-element.707.after), custom_call_target="tpu_custom_call" | custom-call | tf_op jit(solution)/shard_map/while/body/eval_jaxpr/keep/pallas_call | solution.py:145
  181.3 3.1 collective-permute-done.7
  199.4 4.4 %keep.15 = bf16[3,2560,640]{2,1,0:T(8,128)(2,1)S(1)} custom-call(s32[3]{0:T(128)S(1)} %pad_add_fusion.2.scalars, bf16[3,2560,640]{2,1,0:T(8,128)(2,1)} %get-tuple-element.796.src, bf16[64,640]{1,0:T(8,128)(2,1)S(1)} %get-tuple-element.707.after), custom_call_target="tpu_custom_call" | custom-call | tf_op jit(solution)/shard_map/while/body/eval_jaxpr/keep/pallas_call | solution.py:145
  203.8 28.8 %collective-permute-done.4 = bf16[64,640]{1,0:T(8,128)(2,1)S(1)} collective-permute-done((bf16[64,640]{1,0:T(8,128)(2,1)S(1)}, bf16[64,640]{1,0:T(8,128)(2,1)S(1)}, u32[]{:S(2)}, u32[]{:S(2)}) %collective-permute-start.4) | collective-permute-done | bytes 81952 | tf_op jit(solution)/shard_map/while/body/eval_jaxpr/ppermute | solution.py:240
  233.7 2.5 collective-permute-done.7
  238.6 3.0 attend.15
  253.6 4.4 %keep.15 = bf16[3,2560,640]{2,1,0:T(8,128)(2,1)S(1)} custom-call(s32[3]{0:T(128)S(1)} %pad_add_fusion.2.scalars, bf16[3,2560,640]{2,1,0:T(8,128)(2,1)} %get-tuple-element.796.src, bf16[64,640]{1,0:T(8,128)(2,1)S(1)} %get-tuple-element.707.after), custom_call_target="tpu_custom_call" | custom-call | tf_op jit(solution)/shard_map/while/body/eval_jaxpr/keep/pallas_call | solution.py:145
  257.9 4.0 %collective-permute-done.4 = bf16[64,640]{1,0:T(8,128)(2,1)S(1)} collective-permute-done((bf16[64,640]{1,0:T(8,128)(2,1)S(1)}, bf16[64,640]{1,0:T(8,128)(2,1)S(1)}, u32[]{:S(2)}, u32[]{:S(2)}) %collective-permute-start.4) | collective-permute-done | bytes 81952 | tf_op jit(solution)/shard_map/while/body/eval_jaxpr/ppermute | solution.py:240
  262.0 2.8 collective-permute-done.7
  267.2 3.0 attend.15
  282.1 4.4 %keep.15 = bf16[3,2560,640]{2,1,0:T(8,128)(2,1)S(1)} custom-call(s32[3]{0:T(128)S(1)} %pad_add_fusion.2.scalars, bf16[3,2560,640]{2,1,0:T(8,128)(2,1)} %get-tuple-element.796.src, bf16[64,640]{1,0:T(8,128)(2,1)S(1)} %get-tuple-element.707.after), custom_call_target="tpu_custom_call" | custom-call | tf_op jit(solution)/shard_map/while/body/eval_jaxpr/keep/pallas_call | solution.py:145
  286.5 4.2 %collective-permute-done.4 = bf16[64,640]{1,0:T(8,128)(2,1)S(1)} collective-permute-done((bf16[64,640]{1,0:T(8,128)(2,1)S(1)}, bf16[64,640]{1,0:T(8,128)(2,1)S(1)}, u32[]{:S(2)}, u32[]{:S(2)}) %collective-permute-start.4) | collective-permute-done | bytes 81952 | tf_op jit(solution)/shard_map/while/body/eval_jaxpr/ppermute | solution.py:240
  290.8 2.7 collective-permute-done.7
  295.9 3.0 attend.15
  310.9 4.4 %keep.15 = bf16[3,2560,640]{2,1,0:T(8,128)(2,1)S(1)} custom-call(s32[3]{0:T(128)S(1)} %pad_add_fusion.2.scalars, bf16[3,2560,640]{2,1,0:T(8,128)(2,1)} %get-tuple-element.796.src, bf16[64,640]{1,0:T(8,128)(2,1)S(1)} %get-tuple-element.707.after), custom_call_target="tpu_custom_call" | custom-call | tf_op jit(solution)/shard_map/while/body/eval_jaxpr/keep/pallas_call | solution.py:145
  315.2 4.2 %collective-permute-done.4 = bf16[64,640]{1,0:T(8,128)(2,1)S(1)} collective-permute-done((bf16[64,640]{1,0:T(8,128)(2,1)S(1)}, bf16[64,640]{1,0:T(8,128)(2,1)S(1)}, u32[]{:S(2)}, u32[]{:S(2)}) %collective-permute-start.4) | collective-permute-done | bytes 81952 | tf_op jit(solution)/shard_map/while/body/eval_jaxpr/ppermute | solution.py:240
  319.6 2.7 collective-permute-done.7
  324.6 3.0 attend.15
  (415 shorter events, 193.8 us)
Async XLA Ops:
  14.9 14.5 %collective-permute-start.4 = (bf16[64,640]{1,0:T(8,128)(2,1)S(1)}, bf16[64,640]{1,0:T(8,128)(2,1)S(1)}, u32[]{:S(2)}, u32[]{:S(2)}) collective-permute-start(bf16[64,640]{1,0:T(8,128)(2,1)S(1)} %get-tuple-element.707.after), channel_id=1, source_target_pairs={{0,24},{4,28},{8,16},{12,20},{32,56},{36,60},{40,48},{44,52},{64,8... | collective-permute-start | bytes 245768 | tf_op jit(solution)/shard_map/while/body/eval_jaxpr/ppermute | solution.py:240
  16.2 13.8 %collective-permute-start.5 = (bf16[64,640]{1,0:T(8,128)(2,1)S(1)}, bf16[64,640]{1,0:T(8,128)(2,1)S(1)}, u32[]{:S(2)}, u32[]{:S(2)}) collective-permute-start(bf16[64,640]{1,0:T(8,128)(2,1)S(1)} %get-tuple-element.707.after), channel_id=1, source_target_pairs={{0,28},{4,16},{8,20},{12,24},{32,60},{36,48},{40,52},{44,56},{64,9... | collective-permute-start | bytes 245768 | tf_op jit(solution)/shard_map/while/body/eval_jaxpr/ppermute | solution.py:240
  17.5 12.5 %collective-permute-start.6 = (bf16[64,640]{1,0:T(8,128)(2,1)S(1)}, bf16[64,640]{1,0:T(8,128)(2,1)S(1)}, u32[]{:S(2)}, u32[]{:S(2)}) collective-permute-start(bf16[64,640]{1,0:T(8,128)(2,1)S(1)} %get-tuple-element.707.after), channel_id=1, source_target_pairs={{0,16},{4,20},{8,24},{12,28},{32,48},{36,52},{40,56},{44,60},{64,8... | collective-permute-start | bytes 245768 | tf_op jit(solution)/shard_map/while/body/eval_jaxpr/ppermute | solution.py:240
  18.8 13.7 %collective-permute-start.7 = (bf16[64,640]{1,0:T(8,128)(2,1)S(1)}, bf16[64,640]{1,0:T(8,128)(2,1)S(1)}, u32[]{:S(2)}, u32[]{:S(2)}) collective-permute-start(bf16[64,640]{1,0:T(8,128)(2,1)S(1)} %get-tuple-element.707.after), channel_id=1, source_target_pairs={{0,20},{4,24},{8,28},{12,16},{32,52},{36,56},{40,60},{44,48},{64,8... | collective-permute-start | bytes 245768 | tf_op jit(solution)/shard_map/while/body/eval_jaxpr/ppermute | solution.py:240
  42.4 11.5 %collective-permute-start.4 = (bf16[64,640]{1,0:T(8,128)(2,1)S(1)}, bf16[64,640]{1,0:T(8,128)(2,1)S(1)}, u32[]{:S(2)}, u32[]{:S(2)}) collective-permute-start(bf16[64,640]{1,0:T(8,128)(2,1)S(1)} %get-tuple-element.707.after), channel_id=1, source_target_pairs={{0,24},{4,28},{8,16},{12,20},{32,56},{36,60},{40,48},{44,52},{64,8... | collective-permute-start | bytes 245768 | tf_op jit(solution)/shard_map/while/body/eval_jaxpr/ppermute | solution.py:240
  43.7 11.1 %collective-permute-start.5 = (bf16[64,640]{1,0:T(8,128)(2,1)S(1)}, bf16[64,640]{1,0:T(8,128)(2,1)S(1)}, u32[]{:S(2)}, u32[]{:S(2)}) collective-permute-start(bf16[64,640]{1,0:T(8,128)(2,1)S(1)} %get-tuple-element.707.after), channel_id=1, source_target_pairs={{0,28},{4,16},{8,20},{12,24},{32,60},{36,48},{40,52},{44,56},{64,9... | collective-permute-start | bytes 245768 | tf_op jit(solution)/shard_map/while/body/eval_jaxpr/ppermute | solution.py:240
  46.3 11.5 %collective-permute-start.7 = (bf16[64,640]{1,0:T(8,128)(2,1)S(1)}, bf16[64,640]{1,0:T(8,128)(2,1)S(1)}, u32[]{:S(2)}, u32[]{:S(2)}) collective-permute-start(bf16[64,640]{1,0:T(8,128)(2,1)S(1)} %get-tuple-element.707.after), channel_id=1, source_target_pairs={{0,20},{4,24},{8,28},{12,16},{32,52},{36,56},{40,60},{44,48},{64,8... | collective-permute-start | bytes 245768 | tf_op jit(solution)/shard_map/while/body/eval_jaxpr/ppermute | solution.py:240
  67.6 11.9 %collective-permute-start.4 = (bf16[64,640]{1,0:T(8,128)(2,1)S(1)}, bf16[64,640]{1,0:T(8,128)(2,1)S(1)}, u32[]{:S(2)}, u32[]{:S(2)}) collective-permute-start(bf16[64,640]{1,0:T(8,128)(2,1)S(1)} %get-tuple-element.707.after), channel_id=1, source_target_pairs={{0,24},{4,28},{8,16},{12,20},{32,56},{36,60},{40,48},{44,52},{64,8... | collective-permute-start | bytes 245768 | tf_op jit(solution)/shard_map/while/body/eval_jaxpr/ppermute | solution.py:240
  71.5 11.9 %collective-permute-start.7 = (bf16[64,640]{1,0:T(8,128)(2,1)S(1)}, bf16[64,640]{1,0:T(8,128)(2,1)S(1)}, u32[]{:S(2)}, u32[]{:S(2)}) collective-permute-start(bf16[64,640]{1,0:T(8,128)(2,1)S(1)} %get-tuple-element.707.after), channel_id=1, source_target_pairs={{0,20},{4,24},{8,28},{12,16},{32,52},{36,56},{40,60},{44,48},{64,8... | collective-permute-start | bytes 245768 | tf_op jit(solution)/shard_map/while/body/eval_jaxpr/ppermute | solution.py:240
  93.3 11.5 %collective-permute-start.4 = (bf16[64,640]{1,0:T(8,128)(2,1)S(1)}, bf16[64,640]{1,0:T(8,128)(2,1)S(1)}, u32[]{:S(2)}, u32[]{:S(2)}) collective-permute-start(bf16[64,640]{1,0:T(8,128)(2,1)S(1)} %get-tuple-element.707.after), channel_id=1, source_target_pairs={{0,24},{4,28},{8,16},{12,20},{32,56},{36,60},{40,48},{44,52},{64,8... | collective-permute-start | bytes 245768 | tf_op jit(solution)/shard_map/while/body/eval_jaxpr/ppermute | solution.py:240
  97.2 11.5 %collective-permute-start.7 = (bf16[64,640]{1,0:T(8,128)(2,1)S(1)}, bf16[64,640]{1,0:T(8,128)(2,1)S(1)}, u32[]{:S(2)}, u32[]{:S(2)}) collective-permute-start(bf16[64,640]{1,0:T(8,128)(2,1)S(1)} %get-tuple-element.707.after), channel_id=1, source_target_pairs={{0,20},{4,24},{8,28},{12,16},{32,52},{36,56},{40,60},{44,48},{64,8... | collective-permute-start | bytes 245768 | tf_op jit(solution)/shard_map/while/body/eval_jaxpr/ppermute | solution.py:240
  118.5 11.5 %collective-permute-start.4 = (bf16[64,640]{1,0:T(8,128)(2,1)S(1)}, bf16[64,640]{1,0:T(8,128)(2,1)S(1)}, u32[]{:S(2)}, u32[]{:S(2)}) collective-permute-start(bf16[64,640]{1,0:T(8,128)(2,1)S(1)} %get-tuple-element.707.after), channel_id=1, source_target_pairs={{0,24},{4,28},{8,16},{12,20},{32,56},{36,60},{40,48},{44,52},{64,8... | collective-permute-start | bytes 245768 | tf_op jit(solution)/shard_map/while/body/eval_jaxpr/ppermute | solution.py:240
  122.4 11.5 %collective-permute-start.7 = (bf16[64,640]{1,0:T(8,128)(2,1)S(1)}, bf16[64,640]{1,0:T(8,128)(2,1)S(1)}, u32[]{:S(2)}, u32[]{:S(2)}) collective-permute-start(bf16[64,640]{1,0:T(8,128)(2,1)S(1)} %get-tuple-element.707.after), channel_id=1, source_target_pairs={{0,20},{4,24},{8,28},{12,16},{32,52},{36,56},{40,60},{44,48},{64,8... | collective-permute-start | bytes 245768 | tf_op jit(solution)/shard_map/while/body/eval_jaxpr/ppermute | solution.py:240
  143.8 11.5 %collective-permute-start.4 = (bf16[64,640]{1,0:T(8,128)(2,1)S(1)}, bf16[64,640]{1,0:T(8,128)(2,1)S(1)}, u32[]{:S(2)}, u32[]{:S(2)}) collective-permute-start(bf16[64,640]{1,0:T(8,128)(2,1)S(1)} %get-tuple-element.707.after), channel_id=1, source_target_pairs={{0,24},{4,28},{8,16},{12,20},{32,56},{36,60},{40,48},{44,52},{64,8... | collective-permute-start | bytes 245768 | tf_op jit(solution)/shard_map/while/body/eval_jaxpr/ppermute | solution.py:240
  147.7 11.5 %collective-permute-start.7 = (bf16[64,640]{1,0:T(8,128)(2,1)S(1)}, bf16[64,640]{1,0:T(8,128)(2,1)S(1)}, u32[]{:S(2)}, u32[]{:S(2)}) collective-permute-start(bf16[64,640]{1,0:T(8,128)(2,1)S(1)} %get-tuple-element.707.after), channel_id=1, source_target_pairs={{0,20},{4,24},{8,28},{12,16},{32,52},{36,56},{40,60},{44,48},{64,8... | collective-permute-start | bytes 245768 | tf_op jit(solution)/shard_map/while/body/eval_jaxpr/ppermute | solution.py:240
  169.0 11.5 %collective-permute-start.4 = (bf16[64,640]{1,0:T(8,128)(2,1)S(1)}, bf16[64,640]{1,0:T(8,128)(2,1)S(1)}, u32[]{:S(2)}, u32[]{:S(2)}) collective-permute-start(bf16[64,640]{1,0:T(8,128)(2,1)S(1)} %get-tuple-element.707.after), channel_id=1, source_target_pairs={{0,24},{4,28},{8,16},{12,20},{32,56},{36,60},{40,48},{44,52},{64,8... | collective-permute-start | bytes 245768 | tf_op jit(solution)/shard_map/while/body/eval_jaxpr/ppermute | solution.py:240
  172.9 11.5 %collective-permute-start.7 = (bf16[64,640]{1,0:T(8,128)(2,1)S(1)}, bf16[64,640]{1,0:T(8,128)(2,1)S(1)}, u32[]{:S(2)}, u32[]{:S(2)}) collective-permute-start(bf16[64,640]{1,0:T(8,128)(2,1)S(1)} %get-tuple-element.707.after), channel_id=1, source_target_pairs={{0,20},{4,24},{8,28},{12,16},{32,52},{36,56},{40,60},{44,48},{64,8... | collective-permute-start | bytes 245768 | tf_op jit(solution)/shard_map/while/body/eval_jaxpr/ppermute | solution.py:240
  194.2 38.3 %collective-permute-start.4 = (bf16[64,640]{1,0:T(8,128)(2,1)S(1)}, bf16[64,640]{1,0:T(8,128)(2,1)S(1)}, u32[]{:S(2)}, u32[]{:S(2)}) collective-permute-start(bf16[64,640]{1,0:T(8,128)(2,1)S(1)} %get-tuple-element.707.after), channel_id=1, source_target_pairs={{0,24},{4,28},{8,16},{12,20},{32,56},{36,60},{40,48},{44,52},{64,8... | collective-permute-start | bytes 245768 | tf_op jit(solution)/shard_map/while/body/eval_jaxpr/ppermute | solution.py:240
  195.5 38.2 %collective-permute-start.5 = (bf16[64,640]{1,0:T(8,128)(2,1)S(1)}, bf16[64,640]{1,0:T(8,128)(2,1)S(1)}, u32[]{:S(2)}, u32[]{:S(2)}) collective-permute-start(bf16[64,640]{1,0:T(8,128)(2,1)S(1)} %get-tuple-element.707.after), channel_id=1, source_target_pairs={{0,28},{4,16},{8,20},{12,24},{32,60},{36,48},{40,52},{44,56},{64,9... | collective-permute-start | bytes 245768 | tf_op jit(solution)/shard_map/while/body/eval_jaxpr/ppermute | solution.py:240
  196.8 36.9 %collective-permute-start.6 = (bf16[64,640]{1,0:T(8,128)(2,1)S(1)}, bf16[64,640]{1,0:T(8,128)(2,1)S(1)}, u32[]{:S(2)}, u32[]{:S(2)}) collective-permute-start(bf16[64,640]{1,0:T(8,128)(2,1)S(1)} %get-tuple-element.707.after), channel_id=1, source_target_pairs={{0,16},{4,20},{8,24},{12,28},{32,48},{36,52},{40,56},{44,60},{64,8... | collective-permute-start | bytes 245768 | tf_op jit(solution)/shard_map/while/body/eval_jaxpr/ppermute | solution.py:240
  198.1 38.1 %collective-permute-start.7 = (bf16[64,640]{1,0:T(8,128)(2,1)S(1)}, bf16[64,640]{1,0:T(8,128)(2,1)S(1)}, u32[]{:S(2)}, u32[]{:S(2)}) collective-permute-start(bf16[64,640]{1,0:T(8,128)(2,1)S(1)} %get-tuple-element.707.after), channel_id=1, source_target_pairs={{0,20},{4,24},{8,28},{12,16},{32,52},{36,56},{40,60},{44,48},{64,8... | collective-permute-start | bytes 245768 | tf_op jit(solution)/shard_map/while/body/eval_jaxpr/ppermute | solution.py:240
  248.4 13.6 %collective-permute-start.4 = (bf16[64,640]{1,0:T(8,128)(2,1)S(1)}, bf16[64,640]{1,0:T(8,128)(2,1)S(1)}, u32[]{:S(2)}, u32[]{:S(2)}) collective-permute-start(bf16[64,640]{1,0:T(8,128)(2,1)S(1)} %get-tuple-element.707.after), channel_id=1, source_target_pairs={{0,24},{4,28},{8,16},{12,20},{32,56},{36,60},{40,48},{44,52},{64,8... | collective-permute-start | bytes 245768 | tf_op jit(solution)/shard_map/while/body/eval_jaxpr/ppermute | solution.py:240
  249.7 12.3 %collective-permute-start.5 = (bf16[64,640]{1,0:T(8,128)(2,1)S(1)}, bf16[64,640]{1,0:T(8,128)(2,1)S(1)}, u32[]{:S(2)}, u32[]{:S(2)}) collective-permute-start(bf16[64,640]{1,0:T(8,128)(2,1)S(1)} %get-tuple-element.707.after), channel_id=1, source_target_pairs={{0,28},{4,16},{8,20},{12,24},{32,60},{36,48},{40,52},{44,56},{64,9... | collective-permute-start | bytes 245768 | tf_op jit(solution)/shard_map/while/body/eval_jaxpr/ppermute | solution.py:240
  252.3 12.5 %collective-permute-start.7 = (bf16[64,640]{1,0:T(8,128)(2,1)S(1)}, bf16[64,640]{1,0:T(8,128)(2,1)S(1)}, u32[]{:S(2)}, u32[]{:S(2)}) collective-permute-start(bf16[64,640]{1,0:T(8,128)(2,1)S(1)} %get-tuple-element.707.after), channel_id=1, source_target_pairs={{0,20},{4,24},{8,28},{12,16},{32,52},{36,56},{40,60},{44,48},{64,8... | collective-permute-start | bytes 245768 | tf_op jit(solution)/shard_map/while/body/eval_jaxpr/ppermute | solution.py:240
  276.9 13.8 %collective-permute-start.4 = (bf16[64,640]{1,0:T(8,128)(2,1)S(1)}, bf16[64,640]{1,0:T(8,128)(2,1)S(1)}, u32[]{:S(2)}, u32[]{:S(2)}) collective-permute-start(bf16[64,640]{1,0:T(8,128)(2,1)S(1)} %get-tuple-element.707.after), channel_id=1, source_target_pairs={{0,24},{4,28},{8,16},{12,20},{32,56},{36,60},{40,48},{44,52},{64,8... | collective-permute-start | bytes 245768 | tf_op jit(solution)/shard_map/while/body/eval_jaxpr/ppermute | solution.py:240
  278.2 12.6 %collective-permute-start.5 = (bf16[64,640]{1,0:T(8,128)(2,1)S(1)}, bf16[64,640]{1,0:T(8,128)(2,1)S(1)}, u32[]{:S(2)}, u32[]{:S(2)}) collective-permute-start(bf16[64,640]{1,0:T(8,128)(2,1)S(1)} %get-tuple-element.707.after), channel_id=1, source_target_pairs={{0,28},{4,16},{8,20},{12,24},{32,60},{36,48},{40,52},{44,56},{64,9... | collective-permute-start | bytes 245768 | tf_op jit(solution)/shard_map/while/body/eval_jaxpr/ppermute | solution.py:240
  279.5 11.3 %collective-permute-start.6 = (bf16[64,640]{1,0:T(8,128)(2,1)S(1)}, bf16[64,640]{1,0:T(8,128)(2,1)S(1)}, u32[]{:S(2)}, u32[]{:S(2)}) collective-permute-start(bf16[64,640]{1,0:T(8,128)(2,1)S(1)} %get-tuple-element.707.after), channel_id=1, source_target_pairs={{0,16},{4,20},{8,24},{12,28},{32,48},{36,52},{40,56},{44,60},{64,8... | collective-permute-start | bytes 245768 | tf_op jit(solution)/shard_map/while/body/eval_jaxpr/ppermute | solution.py:240
  280.8 12.7 %collective-permute-start.7 = (bf16[64,640]{1,0:T(8,128)(2,1)S(1)}, bf16[64,640]{1,0:T(8,128)(2,1)S(1)}, u32[]{:S(2)}, u32[]{:S(2)}) collective-permute-start(bf16[64,640]{1,0:T(8,128)(2,1)S(1)} %get-tuple-element.707.after), channel_id=1, source_target_pairs={{0,20},{4,24},{8,28},{12,16},{32,52},{36,56},{40,60},{44,48},{64,8... | collective-permute-start | bytes 245768 | tf_op jit(solution)/shard_map/while/body/eval_jaxpr/ppermute | solution.py:240
  305.7 13.8 %collective-permute-start.4 = (bf16[64,640]{1,0:T(8,128)(2,1)S(1)}, bf16[64,640]{1,0:T(8,128)(2,1)S(1)}, u32[]{:S(2)}, u32[]{:S(2)}) collective-permute-start(bf16[64,640]{1,0:T(8,128)(2,1)S(1)} %get-tuple-element.707.after), channel_id=1, source_target_pairs={{0,24},{4,28},{8,16},{12,20},{32,56},{36,60},{40,48},{44,52},{64,8... | collective-permute-start | bytes 245768 | tf_op jit(solution)/shard_map/while/body/eval_jaxpr/ppermute | solution.py:240
  307.0 12.6 %collective-permute-start.5 = (bf16[64,640]{1,0:T(8,128)(2,1)S(1)}, bf16[64,640]{1,0:T(8,128)(2,1)S(1)}, u32[]{:S(2)}, u32[]{:S(2)}) collective-permute-start(bf16[64,640]{1,0:T(8,128)(2,1)S(1)} %get-tuple-element.707.after), channel_id=1, source_target_pairs={{0,28},{4,16},{8,20},{12,24},{32,60},{36,48},{40,52},{44,56},{64,9... | collective-permute-start | bytes 245768 | tf_op jit(solution)/shard_map/while/body/eval_jaxpr/ppermute | solution.py:240
  308.3 11.3 %collective-permute-start.6 = (bf16[64,640]{1,0:T(8,128)(2,1)S(1)}, bf16[64,640]{1,0:T(8,128)(2,1)S(1)}, u32[]{:S(2)}, u32[]{:S(2)}) collective-permute-start(bf16[64,640]{1,0:T(8,128)(2,1)S(1)} %get-tuple-element.707.after), channel_id=1, source_target_pairs={{0,16},{4,20},{8,24},{12,28},{32,48},{36,52},{40,56},{44,60},{64,8... | collective-permute-start | bytes 245768 | tf_op jit(solution)/shard_map/while/body/eval_jaxpr/ppermute | solution.py:240
  309.6 12.7 %collective-permute-start.7 = (bf16[64,640]{1,0:T(8,128)(2,1)S(1)}, bf16[64,640]{1,0:T(8,128)(2,1)S(1)}, u32[]{:S(2)}, u32[]{:S(2)}) collective-permute-start(bf16[64,640]{1,0:T(8,128)(2,1)S(1)} %get-tuple-element.707.after), channel_id=1, source_target_pairs={{0,20},{4,24},{8,28},{12,16},{32,52},{36,56},{40,60},{44,48},{64,8... | collective-permute-start | bytes 245768 | tf_op jit(solution)/shard_map/while/body/eval_jaxpr/ppermute | solution.py:240
  (66 other events, 276.6 us)
